TPU v7x, 32 devices: a whole 2x2x4 slice. The times are simulated.
32 devices in a mesh: grp: 2 (over x), ctr: 16 (over z, y, core).
Axes of the slice: x: 2, y: 2, z: 4, core: 2. Of those that a mesh axis runs over, the one named last changes fastest.
Arguments:
- centres: bfloat16 [6144, 768], P(('grp', 'ctr')), parts along dimension 0
- sample_idx: int32 [1024], P(('grp', 'ctr')), parts along dimension 0, may hold values from 0 to 3071, as said below
- coef: float32 [6144], P(('grp', 'ctr')), parts along dimension 0
- metric_factor: bfloat16 [768, 768], replicated, may hold values from -0.21875 to 0.21875
Outputs:
- metric_new: float32 [1536, 768], P(('grp', 'ctr')), parts along dimension 0
- transformed: float32 [1024, 768], P(('grp', 'ctr')), parts along dimension 0
There are 2 independent parts, one for each index of `grp`. A program takes and returns all parts, laid end to end along the dimension named above; an argument that names none is the same for every part. Nothing has to cross between parts.
Inputs may be any that keep to these rules, and one draw needn't show every extreme that they name: The 32 samples of the k-th aligned block of sample_idx are distinct centres of the k-th block of 192 centres.
All inputs are finite; a program needn't handle non-finite values.
Results may differ from a plain program's by a relative error of at most 0.0031.
Values may be sent and summed in bfloat16 or wider, within the bound.
A program may use at most 128 MiB of HBM per device.

v0:
```python
import jax
import jax.numpy as jnp
from jax import lax
from jax.sharding import PartitionSpec as P


def block_grad(rows_u, v_own, sv_own, coef):
    width = rows_u.shape[1]
    su = jnp.sum(rows_u.astype(jnp.float32) ** 2, axis=1)
    cross = jnp.dot(rows_u, v_own.T, preferred_element_type=jnp.float32)
    dist_sq = jnp.maximum(su[:, None] + sv_own[None, :] - 2.0 * cross, 0.0)
    radius = jnp.sqrt(dist_sq / width + 1.0)
    weight = coef[None, :] * jnp.exp(-radius / 4.0) / (4.0 * width * radius)
    wround = weight.astype(jnp.bfloat16)
    return jnp.dot(wround, v_own, preferred_element_type=jnp.float32) - jnp.sum(weight, axis=1)[
        :, None
    ] * rows_u.astype(jnp.float32)


def local(centres, sample_idx, coef, metric_factor):
    width = centres.shape[1]
    own_count = sample_idx.shape[0]
    devices = lax.axis_size("ctr")
    offset = lax.axis_index("ctr") * centres.shape[0]
    own_rows = jnp.take(centres, sample_idx - offset, axis=0)
    u_own = jnp.dot(own_rows, metric_factor, preferred_element_type=jnp.float32).astype(
        jnp.bfloat16
    )
    v_own = jnp.dot(centres, metric_factor, preferred_element_type=jnp.float32).astype(jnp.bfloat16)
    factor = metric_factor.astype(jnp.float32)
    coef_full = lax.all_gather(coef, "ctr", axis=0, tiled=True)
    piece = lax.all_gather(v_own, "ctr", axis=0, tiled=True)
    sv_piece = jnp.sum(piece.astype(jnp.float32) ** 2, axis=1)
    summed = block_grad(u_own, piece, sv_piece, coef_full)
    grads = jnp.dot(summed, factor.T, precision=lax.Precision.HIGHEST)
    local_outer = jnp.dot(grads.T, grads, precision=lax.Precision.HIGHEST) / (own_count * devices)
    agop = lax.psum(local_outer, "ctr")
    metric_full = agop * width / jnp.trace(agop)
    row_count = width // devices
    metric_rows = lax.dynamic_slice_in_dim(
        metric_full, lax.axis_index("ctr") * row_count, row_count, 0
    )
    transformed = jnp.dot(grads, metric_full, precision=lax.Precision.HIGHEST)
    return (metric_rows, transformed)


def solution(mesh):
    placed = (P(("grp", "ctr"), None), P(("grp", "ctr")), P(("grp", "ctr")), P())
    return jax.shard_map(
        local,
        mesh=mesh,
        in_specs=placed,
        out_specs=(P(("grp", "ctr"), None), P(("grp", "ctr"), None)),
        check_vma=False,
    )
```

profile of v0, /device:TPU:1, one launch (start us, length us, event | category | flops | bytes accessed | tf_op | source)
XLA Modules:
  0.0 197.5 jit_solution(7842170020570275571)
XLA Ops:
  7.2 0.0 copy-start
  7.2 0.0 copy-start.4
  7.2 0.0 copy-start.3
  7.2 0.0 all-gather.2.cloned.1.call-start
  7.2 1.2 copy-done
  8.4 2.1 %convolution_convert_fusion = bf16[192,768]{1,0:T(8,128)(2,1)} fusion(bf16[192,768]{1,0:T(8,128)(2,1)} %param.4, bf16[768,768]{1,0:T(8,128)(2,1)S(1)} %copy-done), kind=kOutput, calls=%fused_computation.12 | convolution fusion | flops 226639872 | bytes 1769472 | tf_op jit(solution)/shard_map/dot_general | solution.py:29
  10.5 0.0 all-gather.2.cloned.1.call-update
  10.5 0.0 all-reduce.3.cloned.1.call-start
  10.6 0.7 compare_and_fusion
  11.3 1.7 gather_fusion
  12.9 0.0 copy-done.4
  12.9 0.6 dynamic-slice
  14.2 0.0 copy-done.3
  14.2 0.3 dynamic-update-slice
  14.5 59.2 %all-reduce = f32[3072]{0:T(1024)S(1)} all-reduce(f32[3072]{0:T(1024)S(1)} %dynamic-update-slice), channel_id=1, replica_groups=mesh['grp'=2,'ctr'=16] {'ctr'}, use_global_device_ids=true, to_apply=%add | all-reduce | flops 3072 | bytes 24576
  73.6 0.5 fusion.6
  74.1 0.0 all-gather.2.cloned.1.call-done
  74.2 0.0 copy-start.1
  74.2 3.5 %multiply_reduce_fusion = f32[3072]{0:T(1024)S(1)} fusion(bf16[3072,768]{1,0:T(8,128)(2,1)} %all-gather.2.cloned.1.call-done), kind=kLoop, calls=%fused_computation.1 | loop fusion | flops 7074816 | bytes 4730880 | tf_op jit(solution)/shard_map/reduce_sum | solution.py:33
  77.6 0.3 copy-done.1
  77.9 1.6 fusion.11
  79.6 0.9 convolution_subtract_fusion
  80.4 1.1 fusion.12
  81.6 3.5 %convolution_multiply_fusion.1 = f32[768,768]{1,0:T(8,128)} fusion(f32[32,768]{1,0:T(8,128)S(1)} %fusion.12), kind=kOutput, calls=%fused_computation.11 | convolution fusion | flops 227082240 | bytes 2457600 | tf_op jit(solution)/shard_map/dot_general | solution.py:36
  85.0 0.0 all-reduce.3.cloned.1.call-update
  85.1 99.5 %all-reduce.3.cloned.1.call-done = f32[768,768]{1,0:T(8,128)} async-done(((f32[768,768]{1,0:T(8,128)}), f32[768,768]{1,0:T(8,128)}) %all-reduce.3.cloned.1.call-update) | async-done | bytes 2359312 | tf_op jit(solution)/shard_map/psum | solution.py:37
  184.6 0.0 copy-start.2
  184.6 2.5 %select_reduce_fusion = f32[]{:T(128)} fusion(f32[768,768]{1,0:T(8,128)} %all-reduce.3.cloned.1.call-done), kind=kLoop, calls=%fused_computation.8 | loop fusion | flops 1769471 | bytes 2359300 | tf_op jit(solution)/shard_map/jit(trace)/reduce_sum | solution.py:38
  187.1 0.0 copy-done.2
  187.1 0.8 multiply_divide_fusion
  187.9 2.1 %fusion.13 = f32[32,768]{1,0:T(8,128)} fusion(f32[32,768]{1,0:T(8,128)S(1)} %fusion.12, f32[768,768]{1,0:T(8,128)S(1)} %multiply_divide_fusion), kind=kOutput, calls=%fused_computation.30 | convolution fusion | flops 226492416 | bytes 2555904 | tf_op jit(solution)/shard_map/dot_general | solution.py:43
  190.0 0.7 constant_dynamic-slice_fusion
  (2 shorter events, 0.0 us)
Async XLA Ops:
  7.2 1.3 copy-start
  7.2 5.8 %copy-start.4 = (u32[32]{0:T(128)S(1)}, u32[32]{0:T(128)}, u32[]{:S(2)}) copy-start(u32[32]{0:T(128)} %constant.52) | copy-start | bytes 388
  7.2 7.0 %copy-start.3 = (f32[192]{0:T(256)S(1)}, f32[192]{0:T(256)}, u32[]{:S(2)}) copy-start(f32[192]{0:T(256)} %param.6) | copy-start | bytes 2308
  7.2 66.9 %all-gather.2.cloned.1.call-start = ((), (), s32[]{:S(2)}) async-start(), calls=%async_computation | async-start | bytes 5013504 | tf_op jit(solution)/shard_map/all_gather | solution.py:32
  10.5 174.0 %all-reduce.3.cloned.1.call-start = ((), (), s32[]{:S(2)}) async-start(), calls=%async_computation.1 | async-start | bytes 4718592 | tf_op jit(solution)/shard_map/psum | solution.py:37
  74.2 3.8 %copy-start.1 = (bf16[3072,768]{1,0:T(8,128)(2,1)S(1)}, bf16[3072,768]{1,0:T(8,128)(2,1)}, u32[]{:S(2)}) copy-start(bf16[3072,768]{1,0:T(8,128)(2,1)} %all-gather.2.cloned.1.call-done) | copy-start | bytes 14155780
  184.6 2.5 %copy-start.2 = (f32[768,768]{1,0:T(8,128)S(1)}, f32[768,768]{1,0:T(8,128)}, u32[]{:S(2)}) copy-start(f32[768,768]{1,0:T(8,128)} %all-reduce.3.cloned.1.call-done) | copy-start | bytes 7077892
Sparse Core Ops, SparseCore 0:
  10.7 56.1 all-gather.1
  85.2 99.3 all-reduce.2
where the time goes:
time: 200 us; the launch traced here: 197 us
  waiting for transfers between devices  99.5 us (50%)
  blocking collectives  59.2 us (30%)
  between operations  14.8 us (7%)
  matrix products  11.8 us (6%)
  other arithmetic  7.48 us (4%)
  local copies, waits for them, and re-layouts  4.68 us (2%)
    psum x1, waiting for transfers between devices, local(): agop = lax.psum(local_outer, 'ctr')  99.5 us
    unnamed x1, blocking collectives  59.2 us
  transfers between devices with their start and end apart: 2, of which 1 were waited for; matrix products, arithmetic and copies ran while one was open for 2% of the time, Pallas kernels for 0%

commit v1 on v0

v1 whole, which is shorter than its diff:
```python
import functools

import jax
import jax.numpy as jnp
from jax import lax
from jax.experimental import pallas as pl
from jax.experimental.pallas import tpu as pltpu
from jax.sharding import PartitionSpec as P

F32 = jnp.float32
BF16 = jnp.bfloat16
NT = (((1,), (1,)), ((), ()))


def split(x):
    high = x.astype(BF16)
    return high, (x - high.astype(F32)).astype(BF16)


def kernel(
    A, B, c_ref, idx_ref, coef_ref, m_ref, metric_ref, out_ref,
    cent, cfs, ucol, vbuf, acc, psend, precv, gall,
    cs_send, cf_send, c_recv, cf_recv, u_send, u_recv, p_send, p_recv,
    gz_send, gy_send, gc_send, g_recv,
):
    own, width = c_ref.shape
    rows = idx_ref.shape[1]
    samples = A * B * 2 * rows
    me = lax.axis_index("ctr")
    c = lax.rem(me, 2)
    b = lax.rem(me // 2, B)
    a = me // (2 * B)

    def dev(a_, b_, c_):
        return {"ctr": (a_ * B + b_) * 2 + c_}

    def copy(src, dst, ssem, rsem, to):
        return pltpu.make_async_remote_copy(
            src_ref=src, dst_ref=dst, send_sem=ssem, recv_sem=rsem,
            device_id=to, device_id_type=pl.DeviceIdType.MESH,
        )

    partner = dev(a, b, 1 - c)
    barrier = pltpu.get_barrier_semaphore()
    peers = [dev(lax.rem(a + k, A), b, c) for k in range(1, A)]
    peers += [dev(a, lax.rem(b + k, B), c) for k in range(1, B)]
    peers += [partner]
    for peer in peers:
        pl.semaphore_signal(barrier, inc=1, device_id=peer, device_id_type=pl.DeviceIdType.MESH)
    pl.semaphore_wait(barrier, len(peers))

    slot = b * 2 + c
    sends = []
    for k in range(1, B):
        to = dev(a, lax.rem(b + k, B), c)
        sends.append(copy(c_ref, cent.at[slot], cs_send.at[k], c_recv.at[slot], to))
        sends.append(copy(coef_ref, cfs.at[slot], cf_send.at[k], cf_recv.at[slot], to))
    sends.append(copy(c_ref, cent.at[slot], cs_send.at[0], c_recv.at[slot], partner))
    sends.append(copy(coef_ref, cfs.at[slot], cf_send.at[0], cf_recv.at[slot], partner))
    for s in sends:
        s.start()

    diag = lax.broadcasted_iota(jnp.int32, (rows, rows), 0) == lax.broadcasted_iota(
        jnp.int32, (rows, rows), 1
    )
    local_idx = (idx_ref[...] - me * own).astype(F32)
    column = jnp.sum(
        jnp.where(diag, jnp.broadcast_to(local_idx, (rows, rows)), 0.0), axis=1, keepdims=True
    )
    places = lax.broadcasted_iota(jnp.int32, (rows, own), 1).astype(F32)
    pick = jnp.where(places == column, 1.0, 0.0).astype(BF16)
    picked = jnp.dot(pick, c_ref[...], preferred_element_type=F32).astype(BF16)
    ucol[a] = jnp.dot(picked, m_ref[...], preferred_element_type=F32).astype(BF16)
    for k in range(1, A):
        s = copy(
            ucol.at[a], ucol.at[a], u_send.at[k], u_recv.at[a], dev(lax.rem(a + k, A), b, c)
        )
        s.start()
        sends.append(s)

    def coords(block):
        vbuf[...] = jnp.dot(block, m_ref[...], preferred_element_type=F32).astype(BF16)

    def arrived(dst, rsem):
        copy(dst, dst, rsem, rsem, partner).wait_recv()

    coords(c_ref[...])
    for k in range(1, A):
        j = lax.rem(a + k, A)
        arrived(ucol.at[j], u_recv.at[j])
    acc[...] = jnp.zeros_like(acc)

    def add_block(coef_row):
        v = vbuf[...]
        u = ucol[...].reshape(A * rows, width)
        uf = u.astype(F32)
        su = jnp.sum(uf * uf, axis=1, keepdims=True)
        vf = v.astype(F32)
        high, low = split(vf * vf)
        ones = jnp.ones((16, width), BF16)
        sv = lax.dot_general(ones, high, NT, preferred_element_type=F32) + lax.dot_general(
            ones, low, NT, preferred_element_type=F32
        )
        cross = lax.dot_general(u, v, NT, preferred_element_type=F32)
        dist_sq = jnp.maximum(su + sv[0:1] - 2.0 * cross, 0.0)
        radius = jnp.sqrt(dist_sq / width + 1.0)
        weight = coef_row * jnp.exp(-radius / 4.0) / (4.0 * width * radius)
        acc[...] += (
            jnp.dot(weight.astype(BF16), v, preferred_element_type=F32)
            - jnp.sum(weight, axis=1, keepdims=True) * uf
        )

    def take(j):
        coords(cent[j])
        add_block(cfs[j])

    def wait_slot(j):
        arrived(cent.at[j], c_recv.at[j])
        arrived(cfs.at[j], cf_recv.at[j])

    add_block(coef_ref[...])
    other = b * 2 + 1 - c
    wait_slot(other)
    take(other)

    def forward(k, to_start):
        j = lax.rem(b + k, B) * 2 + c
        x = copy(cent.at[j], cent.at[j], cs_send.at[B - 1 + k], c_recv.at[j], partner)
        y = copy(cfs.at[j], cfs.at[j], cf_send.at[B - 1 + k], cf_recv.at[j], partner)
        if to_start:
            x.start()
            y.start()
        else:
            x.wait_send()
            y.wait_send()

    def row_step(k, _):
        same = lax.rem(b + k, B) * 2 + c
        wait_slot(same)
        forward(k, True)
        take(same)
        cross = lax.rem(b + k, B) * 2 + 1 - c
        wait_slot(cross)
        take(cross)
        forward(k, False)
        return 0

    lax.fori_loop(1, B, row_step, 0)

    psend[...] = acc[...].astype(BF16).reshape(A, rows, width)
    for k in range(1, A):
        j = lax.rem(a + k, A)
        s = copy(psend.at[j], precv.at[a], p_send.at[k], p_recv.at[a], dev(j, b, c))
        s.start()
        sends.append(s)
    total = acc[pl.ds(pl.multiple_of(a * rows, rows), rows), :]
    for k in range(1, A):
        j = lax.rem(a + k, A)
        arrived(precv.at[j], p_recv.at[j])
        total += precv[j].astype(F32)

    high, low = split(total)
    grads = lax.dot_general(high, m_ref[...], NT, preferred_element_type=F32) + lax.dot_general(
        low, m_ref[...], NT, preferred_element_type=F32
    )

    def place(a_, b_, c_):
        return (c_ * B + b_) * A + a_

    mine = place(a, b, c)
    gall[mine] = grads.astype(BF16)
    for k in range(1, A):
        s = copy(
            gall.at[mine], gall.at[mine], gz_send.at[k], g_recv.at[mine],
            dev(lax.rem(a + k, A), b, c),
        )
        s.start()
        sends.append(s)
    for k in range(A):
        j = place(lax.rem(a + k, A), b, c)
        if k:
            arrived(gall.at[j], g_recv.at[j])
        for q in range(1, B):
            s = copy(
                gall.at[j], gall.at[j], gy_send.at[k * B + q], g_recv.at[j],
                dev(a, lax.rem(b + q, B), c),
            )
            s.start()
            sends.append(s)
        s = copy(gall.at[j], gall.at[j], gc_send.at[k], g_recv.at[j], partner)
        s.start()
        sends.append(s)
    for k in range(A):
        for q in range(1, B):
            j = place(lax.rem(a + k, A), lax.rem(b + q, B), c)
            arrived(gall.at[j], g_recv.at[j])
            s = copy(gall.at[j], gall.at[j], gc_send.at[q * A + k], g_recv.at[j], partner)
            s.start()
            sends.append(s)
    for k in range(A):
        for q in range(B):
            j = place(lax.rem(a + k, A), lax.rem(b + q, B), 1 - c)
            arrived(gall.at[j], g_recv.at[j])

    metric_rows = metric_ref.shape[0]
    padded = -(-metric_rows // 16) * 16

    def squares(i, t):
        g = gall[i].astype(F32)
        return t + g * g

    square = lax.fori_loop(0, A * B * 2, squares, jnp.zeros((rows, width), F32))
    trace = jnp.sum(jnp.sum(square, axis=1, keepdims=True), axis=0, keepdims=True) / samples

    full = gall[...].reshape(samples, width)
    line = lax.broadcasted_iota(jnp.int32, (padded, width), 0) + me * metric_rows
    choose = jnp.where(
        line == lax.broadcasted_iota(jnp.int32, (padded, width), 1), 1.0, 0.0
    ).astype(BF16)
    ghigh, glow = split(grads)
    left = jnp.concatenate([choose, ghigh, glow], axis=0)
    inner = lax.dot_general(left, full, NT, preferred_element_type=F32)
    gram = inner[padded : padded + rows] + inner[padded + rows :]
    phigh, plow = split((gram / samples) * width / trace)
    left = jnp.concatenate([inner[:padded].astype(BF16), phigh, plow], axis=0)
    result = jnp.dot(left, full, preferred_element_type=F32)
    metric_ref[...] = (result[:metric_rows] / samples) * width / trace
    out_ref[...] = result[padded : padded + rows] + result[padded + rows :]

    for s in sends:
        s.wait_send()


def local(A, B, centres, sample_idx, coef, metric_factor):
    own, width = centres.shape
    rows = sample_idx.shape[0]
    n = A * B * 2
    dma = lambda k: pltpu.SemaphoreType.DMA((k,))
    vmem = pl.BlockSpec(memory_space=pltpu.VMEM)
    return pl.pallas_call(
        functools.partial(kernel, A, B),
        out_shape=(
            jax.ShapeDtypeStruct((width // n, width), F32),
            jax.ShapeDtypeStruct((rows, width), F32),
        ),
        in_specs=[vmem] * 4,
        out_specs=(vmem, vmem),
        scratch_shapes=[
            pltpu.VMEM((2 * B, own, width), BF16),
            pltpu.VMEM((2 * B, 1, own), F32),
            pltpu.VMEM((A, rows, width), BF16),
            pltpu.VMEM((own, width), BF16),
            pltpu.VMEM((A * rows, width), F32),
            pltpu.VMEM((A, rows, width), BF16),
            pltpu.VMEM((A, rows, width), BF16),
            pltpu.VMEM((n, rows, width), BF16),
            dma(2 * B), dma(2 * B), dma(2 * B), dma(2 * B),
            dma(A), dma(A), dma(A), dma(A),
            dma(A), dma(A * B), dma(A * B), dma(n),
        ],
        compiler_params=pltpu.CompilerParams(collective_id=0, has_side_effects=True),
    )(centres, sample_idx.reshape(1, rows), coef.reshape(1, own), metric_factor)


def solution(mesh):
    chips = mesh.shape["ctr"] // 2
    A = 1
    while A * A < chips:
        A *= 2
    B = chips // A
    placed = (P(("grp", "ctr"), None), P(("grp", "ctr")), P(("grp", "ctr")), P())
    return jax.shard_map(
        functools.partial(local, A, B),
        mesh=mesh,
        in_specs=placed,
        out_specs=(P(("grp", "ctr"), None), P(("grp", "ctr"), None)),
        check_vma=False,
    )
```

time: 200 us -> 40.4 us (0.20); the launches traced: 197 us -> 40.2 us
  waiting for transfers between devices: 99.5 us -> 0 us
  blocking collectives: 59.2 us -> 0 us
  Pallas kernels: 0 us -> 36.4 us
  between operations: 14.8 us -> 0.64 us
  matrix products: 11.8 us -> 0 us
  other arithmetic: 7.48 us -> 0 us
    psum x1 -> x0, waiting for transfers between devices: 99.5 us -> none  [local(): agop = lax.psum(local_outer, 'ctr')]
    unnamed x1 -> x0, blocking collectives: 59.2 us -> none
    pallas_call x0 -> x1, Pallas kernels: none -> 36.4 us  [local(): pl.pallas_call(functools.partial(kernel, A, B), out_shape=(jax.ShapeDtype...]
    dot_general x7 -> x0, matrix products: 11.8 us -> none  [the longest x1 3.49 us: local(): jnp.dot(grads.T, grads, precision=lax.Precision.HIGHEST)]
    reduce_sum x2 -> x0, other arithmetic: 6 us -> none  [the longest x1 3.48 us: local(): sv_piece = jnp.sum(piece.astype(jnp.float32) ** 2, axis=1)]
  transfers between devices with their start and end apart: 2 -> 0, of which waited for: 1 -> 0; matrix products, arithmetic and copies ran while one was open for 2% -> 0% of each run, Pallas kernels for 0% -> 0%
where the time goes in v1:
time: 40.4 us; the launch traced here: 40.2 us
  Pallas kernels  36.4 us (90%)
  local copies, waits for them, and re-layouts  3.12 us (8%)
  between operations  0.64 us (2%)
    pallas_call x1, Pallas kernels, local(): pl.pallas_call(functools.partial(kernel, A, B), out_shape=(jax.ShapeDtype...  36.4 us
    unnamed x2, local copies, waits for them, and re-layouts  3.12 us

profile of v1, /device:TPU:1, one launch (start us, length us, event | category | flops | bytes accessed | tf_op | source)
XLA Modules:
  0.0 40.2 jit_solution(4502258857376594938)
XLA Ops:
  0.6 36.4 %shard_map.59 = (f32[48,768]{1,0:T(8,128)}, f32[32,768]{1,0:T(8,128)}) custom-call(bf16[192,768]{1,0:T(8,128)(2,1)} %c_ref.1, s32[1,32]{1,0:T(1,128)} %bitcast.3, f32[1,192]{1,0:T(1,128)} %bitcast.2, bf16[768,768]{1,0:T(8,128)(2,1)} %m_ref.1), custom_call_target="tpu_custom_call" | custom-call | tf_op jit(solution)/shard_map/pallas_call | solution.py:240
  37.0 1.6 %copy.8 = f32[48,768]{1,0:T(8,128)} copy(f32[48,768]{1,0:T(8,128)} %get-tuple-element.4) | data formatting | bytes 294912
  38.6 1.5 %copy.9 = f32[32,768]{1,0:T(8,128)} copy(f32[32,768]{1,0:T(8,128)} %get-tuple-element.5) | data formatting | bytes 196608

commit v2 on v1

--- a/solution.py
+++ b/solution.py
@@ -12,20 +12,27 @@
 NT = (((1,), (1,)), ((), ()))
 
 
+def parts(own):
+    first = own // 256 * 128 + 128 if own > 128 else own
+    return [(0, first)] + ([(first, own - first)] if first < own else [])
+
+
 def split(x):
     high = x.astype(BF16)
     return high, (x - high.astype(F32)).astype(BF16)
 
 
 def kernel(
-    A, B, c_ref, idx_ref, coef_ref, m_ref, metric_ref, out_ref,
-    cent, cfs, ucol, vbuf, acc, psend, precv, gall,
+    A, B, c_hbm, idx_hbm, coef_hbm, m_hbm, gall, grads_ref,
+    c_ref, idx_ref, coef_ref, m_ref,
+    cent, cfs, ucol, vbuf, acc, psend, precv,
     cs_send, cf_send, c_recv, cf_recv, u_send, u_recv, p_send, p_recv,
-    gz_send, gy_send, gc_send, g_recv,
+    gz_send, gy_send, gc_send, g_recv, load,
 ):
     own, width = c_ref.shape
     rows = idx_ref.shape[1]
-    samples = A * B * 2 * rows
+    cuts = parts(own)
+    H = len(cuts)
     me = lax.axis_index("ctr")
     c = lax.rem(me, 2)
     b = lax.rem(me // 2, B)
@@ -47,22 +54,50 @@
     peers += [partner]
     for peer in peers:
         pl.semaphore_signal(barrier, inc=1, device_id=peer, device_id_type=pl.DeviceIdType.MESH)
+    loads = [
+        pltpu.make_async_copy(src, dst, load.at[k])
+        for k, (src, dst) in enumerate(
+            [(idx_hbm, idx_ref), (c_hbm, c_ref), (m_hbm, m_ref), (coef_hbm, coef_ref)]
+        )
+    ]
+    for item in loads:
+        item.start()
     pl.semaphore_wait(barrier, len(peers))
 
     slot = b * 2 + c
     sends = []
+
+    def piece(ref, h):
+        return ref.at[pl.ds(cuts[h][0], cuts[h][1])]
+
     for k in range(1, B):
         to = dev(a, lax.rem(b + k, B), c)
-        sends.append(copy(c_ref, cent.at[slot], cs_send.at[k], c_recv.at[slot], to))
-        sends.append(copy(coef_ref, cfs.at[slot], cf_send.at[k], cf_recv.at[slot], to))
-    sends.append(copy(c_ref, cent.at[slot], cs_send.at[0], c_recv.at[slot], partner))
-    sends.append(copy(coef_ref, cfs.at[slot], cf_send.at[0], cf_recv.at[slot], partner))
+        sends.append(copy(coef_hbm, cfs.at[slot], cf_send.at[k], cf_recv.at[slot], to))
+    for h in range(H):
+        for k in range(1, B):
+            to = dev(a, lax.rem(b + k, B), c)
+            sends.append(copy(
+                piece(c_hbm, h), piece(cent.at[slot], h), cs_send.at[k * H + h],
+                c_recv.at[slot * H + h], to,
+            ))
+    sends.append(copy(coef_hbm, cfs.at[slot], cf_send.at[0], cf_recv.at[slot], partner))
+    for h in range(H):
+        sends.append(copy(
+            piece(c_hbm, h), piece(cent.at[slot], h), cs_send.at[h], c_recv.at[slot * H + h],
+            partner,
+        ))
     for s in sends:
         s.start()
+    sign = 2 * (a // (A // 2)) - 1
+
+    def along(k):
+        return lax.rem(a + sign * k + A, A)
 
     diag = lax.broadcasted_iota(jnp.int32, (rows, rows), 0) == lax.broadcasted_iota(
         jnp.int32, (rows, rows), 1
     )
+    loads[0].wait()
+    loads[1].wait()
     local_idx = (idx_ref[...] - me * own).astype(F32)
     column = jnp.sum(
         jnp.where(diag, jnp.broadcast_to(local_idx, (rows, rows)), 0.0), axis=1, keepdims=True
@@ -70,28 +105,31 @@
     places = lax.broadcasted_iota(jnp.int32, (rows, own), 1).astype(F32)
     pick = jnp.where(places == column, 1.0, 0.0).astype(BF16)
     picked = jnp.dot(pick, c_ref[...], preferred_element_type=F32).astype(BF16)
+    loads[2].wait()
     ucol[a] = jnp.dot(picked, m_ref[...], preferred_element_type=F32).astype(BF16)
     for k in range(1, A):
         s = copy(
-            ucol.at[a], ucol.at[a], u_send.at[k], u_recv.at[a], dev(lax.rem(a + k, A), b, c)
+            ucol.at[a], ucol.at[a], u_send.at[k], u_recv.at[a], dev(along(k), b, c)
         )
         s.start()
         sends.append(s)
 
     def coords(block):
-        vbuf[...] = jnp.dot(block, m_ref[...], preferred_element_type=F32).astype(BF16)
+        vbuf[: block.shape[0]] = jnp.dot(
+            block, m_ref[...], preferred_element_type=F32
+        ).astype(BF16)
 
     def arrived(dst, rsem):
         copy(dst, dst, rsem, rsem, partner).wait_recv()
 
     coords(c_ref[...])
     for k in range(1, A):
-        j = lax.rem(a + k, A)
+        j = along(k)
         arrived(ucol.at[j], u_recv.at[j])
     acc[...] = jnp.zeros_like(acc)
 
     def add_block(coef_row):
-        v = vbuf[...]
+        v = vbuf[: coef_row.shape[1]]
         u = ucol[...].reshape(A * rows, width)
         uf = u.astype(F32)
         su = jnp.sum(uf * uf, axis=1, keepdims=True)
@@ -110,52 +148,61 @@
             - jnp.sum(weight, axis=1, keepdims=True) * uf
         )
 
-    def take(j):
-        coords(cent[j])
-        add_block(cfs[j])
-
-    def wait_slot(j):
-        arrived(cent.at[j], c_recv.at[j])
-        arrived(cfs.at[j], cf_recv.at[j])
-
+    def take(j, h):
+        first, count = cuts[h]
+        coords(cent[j, first : first + count])
+        add_block(cfs[j][:, first : first + count])
+
+    def wait_piece(j, h):
+        x = piece(cent.at[j], h)
+        arrived(x, c_recv.at[j * H + h])
+
+    loads[3].wait()
     add_block(coef_ref[...])
     other = b * 2 + 1 - c
-    wait_slot(other)
-    take(other)
-
-    def forward(k, to_start):
-        j = lax.rem(b + k, B) * 2 + c
-        x = copy(cent.at[j], cent.at[j], cs_send.at[B - 1 + k], c_recv.at[j], partner)
-        y = copy(cfs.at[j], cfs.at[j], cf_send.at[B - 1 + k], cf_recv.at[j], partner)
-        if to_start:
-            x.start()
-            y.start()
-        else:
-            x.wait_send()
-            y.wait_send()
+    arrived(cfs.at[other], cf_recv.at[other])
+    for h in range(H):
+        wait_piece(other, h)
+    coords(cent[other])
+    add_block(cfs[other])
 
     def row_step(k, _):
         same = lax.rem(b + k, B) * 2 + c
-        wait_slot(same)
-        forward(k, True)
-        take(same)
         cross = lax.rem(b + k, B) * 2 + 1 - c
-        wait_slot(cross)
-        take(cross)
-        forward(k, False)
+        hops = []
+        arrived(cfs.at[same], cf_recv.at[same])
+        hops.append(copy(
+            cfs.at[same], cfs.at[same], cf_send.at[B - 1 + k], cf_recv.at[same], partner
+        ))
+        hops[0].start()
+        for h in range(H):
+            wait_piece(same, h)
+            hop = copy(
+                piece(cent.at[same], h), piece(cent.at[same], h),
+                cs_send.at[(B - 1 + k) * H + h], c_recv.at[same * H + h], partner,
+            )
+            hop.start()
+            hops.append(hop)
+            take(same, h)
+            if h == 0:
+                arrived(cfs.at[cross], cf_recv.at[cross])
+            wait_piece(cross, h)
+            take(cross, h)
+        for hop in hops:
+            hop.wait_send()
         return 0
 
     lax.fori_loop(1, B, row_step, 0)
 
     psend[...] = acc[...].astype(BF16).reshape(A, rows, width)
     for k in range(1, A):
-        j = lax.rem(a + k, A)
+        j = along(k)
         s = copy(psend.at[j], precv.at[a], p_send.at[k], p_recv.at[a], dev(j, b, c))
         s.start()
         sends.append(s)
     total = acc[pl.ds(pl.multiple_of(a * rows, rows), rows), :]
     for k in range(1, A):
-        j = lax.rem(a + k, A)
+        j = along(k)
         arrived(precv.at[j], p_recv.at[j])
         total += precv[j].astype(F32)
 
@@ -169,15 +216,16 @@
 
     mine = place(a, b, c)
     gall[mine] = grads.astype(BF16)
+    grads_ref[...] = grads
     for k in range(1, A):
         s = copy(
             gall.at[mine], gall.at[mine], gz_send.at[k], g_recv.at[mine],
-            dev(lax.rem(a + k, A), b, c),
+            dev(along(k), b, c),
         )
         s.start()
         sends.append(s)
     for k in range(A):
-        j = place(lax.rem(a + k, A), b, c)
+        j = place(along(k), b, c)
         if k:
             arrived(gall.at[j], g_recv.at[j])
         for q in range(1, B):
@@ -192,7 +240,7 @@
         sends.append(s)
     for k in range(A):
         for q in range(1, B):
-            j = place(lax.rem(a + k, A), lax.rem(b + q, B), c)
+            j = place(along(k), lax.rem(b + q, B), c)
             arrived(gall.at[j], g_recv.at[j])
             s = copy(gall.at[j], gall.at[j], gc_send.at[q * A + k], g_recv.at[j], partner)
             s.start()
@@ -202,6 +250,15 @@
             j = place(lax.rem(a + k, A), lax.rem(b + q, B), 1 - c)
             arrived(gall.at[j], g_recv.at[j])
 
+    for s in sends:
+        s.wait_send()
+
+
+def finish(gall, grads_ref, metric_ref, out_ref):
+    blocks, rows, width = gall.shape
+    samples = blocks * rows
+    me = lax.axis_index("ctr")
+    grads = grads_ref[...]
     metric_rows = metric_ref.shape[0]
     padded = -(-metric_rows // 16) * 16
 
@@ -209,7 +266,7 @@
         g = gall[i].astype(F32)
         return t + g * g
 
-    square = lax.fori_loop(0, A * B * 2, squares, jnp.zeros((rows, width), F32))
+    square = lax.fori_loop(0, blocks, squares, jnp.zeros((rows, width), F32))
     trace = jnp.sum(jnp.sum(square, axis=1, keepdims=True), axis=0, keepdims=True) / samples
 
     full = gall[...].reshape(samples, width)
@@ -227,9 +284,6 @@
     metric_ref[...] = (result[:metric_rows] / samples) * width / trace
     out_ref[...] = result[padded : padded + rows] + result[padded + rows :]
 
-    for s in sends:
-        s.wait_send()
-
 
 def local(A, B, centres, sample_idx, coef, metric_factor):
     own, width = centres.shape
@@ -237,15 +291,19 @@
     n = A * B * 2
     dma = lambda k: pltpu.SemaphoreType.DMA((k,))
     vmem = pl.BlockSpec(memory_space=pltpu.VMEM)
-    return pl.pallas_call(
+    H = len(parts(own))
+    limit = 67043328 - (n * 2 + 4) * rows * width
+    hbm = pl.BlockSpec(memory_space=pltpu.HBM)
+    gall, grads = pl.pallas_call(
         functools.partial(kernel, A, B),
-        out_shape=(
-            jax.ShapeDtypeStruct((width // n, width), F32),
-            jax.ShapeDtypeStruct((rows, width), F32),
-        ),
-        in_specs=[vmem] * 4,
+        out_shape=(pltpu.VMEM((n, rows, width), BF16), pltpu.VMEM((rows, width), F32)),
+        in_specs=[hbm] * 4,
         out_specs=(vmem, vmem),
         scratch_shapes=[
+            pltpu.VMEM((own, width), BF16),
+            pltpu.VMEM((1, rows), jnp.int32),
+            pltpu.VMEM((1, own), F32),
+            pltpu.VMEM((width, width), BF16),
             pltpu.VMEM((2 * B, own, width), BF16),
             pltpu.VMEM((2 * B, 1, own), F32),
             pltpu.VMEM((A, rows, width), BF16),
@@ -253,13 +311,24 @@
             pltpu.VMEM((A * rows, width), F32),
             pltpu.VMEM((A, rows, width), BF16),
             pltpu.VMEM((A, rows, width), BF16),
-            pltpu.VMEM((n, rows, width), BF16),
-            dma(2 * B), dma(2 * B), dma(2 * B), dma(2 * B),
+            dma(2 * B * H), dma(2 * B), dma(2 * B * H), dma(2 * B),
             dma(A), dma(A), dma(A), dma(A),
-            dma(A), dma(A * B), dma(A * B), dma(n),
+            dma(A), dma(A * B), dma(A * B), dma(n), dma(4),
         ],
-        compiler_params=pltpu.CompilerParams(collective_id=0, has_side_effects=True),
+        compiler_params=pltpu.CompilerParams(
+            collective_id=0, has_side_effects=True, vmem_limit_bytes=limit
+        ),
     )(centres, sample_idx.reshape(1, rows), coef.reshape(1, own), metric_factor)
+    return pl.pallas_call(
+        finish,
+        out_shape=(
+            jax.ShapeDtypeStruct((width // n, width), F32),
+            jax.ShapeDtypeStruct((rows, width), F32),
+        ),
+        in_specs=[vmem] * 2,
+        out_specs=(vmem, vmem),
+        compiler_params=pltpu.CompilerParams(vmem_limit_bytes=40 * 2**20),
+    )(gall, grads)
 
 
 def solution(mesh):

time: 40.4 us -> 36.6 us (0.906)
  local copies, waits for them, and re-layouts: 3.12 us -> 0 us
  Pallas kernels: 36.4 us -> 35.7 us
    unnamed x2 -> x0, local copies, waits for them, and re-layouts: 3.12 us -> none
    pallas_call x1 -> x2, Pallas kernels: 36.4 us -> 35.7 us  [the longest x1 34.2 us: local(): pl.pallas_call(functools.partial(kernel, A, B), out_shape=(pltpu.VMEM((n,...]
where the time goes in v2:
time: 36.6 us; the launch traced here: 36.4 us
  Pallas kernels  35.7 us (98%)
  between operations  0.64 us (2%)
    pallas_call x1, Pallas kernels, local(): pl.pallas_call(functools.partial(kernel, A, B), out_shape=(pltpu.VMEM((n,...  34.2 us
    pallas_call x1, Pallas kernels, local(): pl.pallas_call(finish, out_shape=(jax.ShapeDtypeStruct((width // n, width...  1.57 us

profile of v2, /device:TPU:1, one launch (start us, length us, event | category | flops | bytes accessed | tf_op | source)
XLA Modules:
  0.0 36.4 jit_solution(51032654477139027)
XLA Ops:
  0.6 34.2 %shard_map.59 = (bf16[16,32,768]{2,1,0:T(8,128)(2,1)S(1)}, f32[32,768]{1,0:T(8,128)S(1)}) custom-call(bf16[192,768]{1,0:T(8,128)(2,1)} %c_hbm.1, s32[1,32]{1,0:T(1,128)} %bitcast.3, f32[1,192]{1,0:T(1,128)} %bitcast.2, bf16[768,768]{1,0:T(8,128)(2,1)} %m_hbm.1), custom_call_target="tpu_custom_call" | custom-call | tf_op jit(solution)/shard_map/pallas_call | solution.py:297
  34.8 1.6 %shard_map.60 = (f32[48,768]{1,0:T(8,128)}, f32[32,768]{1,0:T(8,128)}) custom-call(bf16[16,32,768]{2,1,0:T(8,128)(2,1)S(1)} %get-tuple-element.4.gall, f32[32,768]{1,0:T(8,128)S(1)} %get-tuple-element.5.grads_ref), custom_call_target="tpu_custom_call" | custom-call | tf_op jit(solution)/shard_map/pallas_call | solution.py:322

commit v3 on v2

--- a/solution.py
+++ b/solution.py
@@ -13,7 +13,7 @@
 
 
 def parts(own):
-    first = own // 256 * 128 + 128 if own > 128 else own
+    first = own
     return [(0, first)] + ([(first, own - first)] if first < own else [])
 
 
@@ -25,7 +25,7 @@
 def kernel(
     A, B, c_hbm, idx_hbm, coef_hbm, m_hbm, gall, grads_ref,
     c_ref, idx_ref, coef_ref, m_ref,
-    cent, cfs, ucol, vbuf, acc, psend, precv,
+    cent, cfs, ucol, vbuf, acc, su_ref, wsum, psend, precv,
     cs_send, cf_send, c_recv, cf_recv, u_send, u_recv, p_send, p_recv,
     gz_send, gy_send, gc_send, g_recv, load,
 ):
@@ -115,24 +115,48 @@
         sends.append(s)
 
     def coords(block):
-        vbuf[: block.shape[0]] = jnp.dot(
-            block, m_ref[...], preferred_element_type=F32
-        ).astype(BF16)
+        return jnp.dot(block, m_ref[...], preferred_element_type=F32).astype(BF16)
 
     def arrived(dst, rsem):
         copy(dst, dst, rsem, rsem, partner).wait_recv()
 
-    coords(c_ref[...])
+    def wait_piece(j, h):
+        arrived(piece(cent.at[j], h), c_recv.at[j * H + h])
+
+    def relay(k, h):
+        j = lax.rem(b + k, B) * 2 + c
+        wait_piece(j, h)
+        first, count = cuts[h]
+        cent[j, first : first + count] = coords(cent[j, first : first + count])
+        hop = copy(
+            piece(cent.at[j], h), piece(cent.at[j], h),
+            cs_send.at[(B - 1 + k) * H + h], c_recv.at[j * H + h], partner,
+        )
+        hop.start()
+        hops = [hop]
+        if h == 0:
+            arrived(cfs.at[j], cf_recv.at[j])
+            hop = copy(cfs.at[j], cfs.at[j], cf_send.at[B - 1 + k], cf_recv.at[j], partner)
+            hop.start()
+            hops.append(hop)
+        return hops
+
+    vbuf[...] = coords(c_ref[...])
+    other = b * 2 + 1 - c
+    for h in range(H):
+        wait_piece(other, h)
+    cent[other] = coords(cent[other])
+    early = relay(1, 0)
     for k in range(1, A):
         j = along(k)
         arrived(ucol.at[j], u_recv.at[j])
+    uf = ucol[...].reshape(A * rows, width).astype(F32)
+    su_ref[...] = jnp.sum(uf * uf, axis=1, keepdims=True)
     acc[...] = jnp.zeros_like(acc)
-
-    def add_block(coef_row):
-        v = vbuf[: coef_row.shape[1]]
+    wsum[...] = jnp.zeros_like(wsum)
+
+    def add_block(v, coef_row):
         u = ucol[...].reshape(A * rows, width)
-        uf = u.astype(F32)
-        su = jnp.sum(uf * uf, axis=1, keepdims=True)
         vf = v.astype(F32)
         high, low = split(vf * vf)
         ones = jnp.ones((16, width), BF16)
@@ -140,63 +164,43 @@
             ones, low, NT, preferred_element_type=F32
         )
         cross = lax.dot_general(u, v, NT, preferred_element_type=F32)
-        dist_sq = jnp.maximum(su + sv[0:1] - 2.0 * cross, 0.0)
+        dist_sq = jnp.maximum(su_ref[...] + sv[0:1] - 2.0 * cross, 0.0)
         radius = jnp.sqrt(dist_sq / width + 1.0)
         weight = coef_row * jnp.exp(-radius / 4.0) / (4.0 * width * radius)
-        acc[...] += (
-            jnp.dot(weight.astype(BF16), v, preferred_element_type=F32)
-            - jnp.sum(weight, axis=1, keepdims=True) * uf
-        )
-
-    def take(j, h):
-        first, count = cuts[h]
-        coords(cent[j, first : first + count])
-        add_block(cfs[j][:, first : first + count])
-
-    def wait_piece(j, h):
-        x = piece(cent.at[j], h)
-        arrived(x, c_recv.at[j * H + h])
+        acc[...] += jnp.dot(weight.astype(BF16), v, preferred_element_type=F32)
+        wsum[...] += jnp.sum(weight, axis=1, keepdims=True)
 
     loads[3].wait()
-    add_block(coef_ref[...])
-    other = b * 2 + 1 - c
+    add_block(vbuf[...], coef_ref[...])
     arrived(cfs.at[other], cf_recv.at[other])
-    for h in range(H):
-        wait_piece(other, h)
-    coords(cent[other])
-    add_block(cfs[other])
-
-    def row_step(k, _):
+    add_block(cent[other], cfs[other])
+
+    def row_step(k, hops):
         same = lax.rem(b + k, B) * 2 + c
         cross = lax.rem(b + k, B) * 2 + 1 - c
-        hops = []
-        arrived(cfs.at[same], cf_recv.at[same])
-        hops.append(copy(
-            cfs.at[same], cfs.at[same], cf_send.at[B - 1 + k], cf_recv.at[same], partner
-        ))
-        hops[0].start()
+        for h in range(1, H):
+            hops = hops + relay(k, h)
+        add_block(cent[same], cfs[same])
+        arrived(cfs.at[cross], cf_recv.at[cross])
         for h in range(H):
-            wait_piece(same, h)
-            hop = copy(
-                piece(cent.at[same], h), piece(cent.at[same], h),
-                cs_send.at[(B - 1 + k) * H + h], c_recv.at[same * H + h], partner,
-            )
-            hop.start()
-            hops.append(hop)
-            take(same, h)
-            if h == 0:
-                arrived(cfs.at[cross], cf_recv.at[cross])
             wait_piece(cross, h)
-            take(cross, h)
-        for hop in hops:
+        add_block(cent[cross], cfs[cross])
+        return hops
+
+    sends += row_step(1, early)
+
+    def later_step(k, _):
+        for hop in row_step(k, relay(k, 0)):
             hop.wait_send()
         return 0
 
-    lax.fori_loop(1, B, row_step, 0)
+    if B > 2:
+        lax.fori_loop(2, B, later_step, 0)
+    acc[...] -= wsum[...] * ucol[...].reshape(A * rows, width).astype(F32)
 
     psend[...] = acc[...].astype(BF16).reshape(A, rows, width)
     for k in range(1, A):
-        j = along(k)
+        j = lax.rem(a + k, A)
         s = copy(psend.at[j], precv.at[a], p_send.at[k], p_recv.at[a], dev(j, b, c))
         s.start()
         sends.append(s)
@@ -309,6 +313,8 @@
             pltpu.VMEM((A, rows, width), BF16),
             pltpu.VMEM((own, width), BF16),
             pltpu.VMEM((A * rows, width), F32),
+            pltpu.VMEM((A * rows, 1), F32),
+            pltpu.VMEM((A * rows, 1), F32),
             pltpu.VMEM((A, rows, width), BF16),
             pltpu.VMEM((A, rows, width), BF16),
             dma(2 * B * H), dma(2 * B), dma(2 * B * H), dma(2 * B),

time: 36.6 us -> 34.9 us (0.954)
  Pallas kernels: 35.7 us -> 34.1 us
    pallas_call x1, Pallas kernels: 34.2 us -> 32.5 us  [local(): pl.pallas_call(functools.partial(kernel, A, B), out_shape=(pltpu.VMEM((n,...]
where the time goes in v3:
time: 34.9 us; the launch traced here: 34.7 us
  Pallas kernels  34.1 us (98%)
  between operations  0.64 us (2%)
    pallas_call x1, Pallas kernels, local(): pl.pallas_call(functools.partial(kernel, A, B), out_shape=(pltpu.VMEM((n,...  32.5 us
    pallas_call x1, Pallas kernels, local(): pl.pallas_call(finish, out_shape=(jax.ShapeDtypeStruct((width // n, width...  1.57 us

profile of v3, /device:TPU:1, one launch (start us, length us, event | category | flops | bytes accessed | tf_op | source)
XLA Modules:
  0.0 34.7 jit_solution(9269217786007945126)
XLA Ops:
  0.6 32.5 %shard_map.59 = (bf16[16,32,768]{2,1,0:T(8,128)(2,1)S(1)}, f32[32,768]{1,0:T(8,128)S(1)}) custom-call(bf16[192,768]{1,0:T(8,128)(2,1)} %c_hbm.1, s32[1,32]{1,0:T(1,128)} %bitcast.3, f32[1,192]{1,0:T(1,128)} %bitcast.2, bf16[768,768]{1,0:T(8,128)(2,1)} %m_hbm.1), custom_call_target="tpu_custom_call" | custom-call | tf_op jit(solution)/shard_map/pallas_call | solution.py:301
  33.1 1.6 %shard_map.60 = (f32[48,768]{1,0:T(8,128)}, f32[32,768]{1,0:T(8,128)}) custom-call(bf16[16,32,768]{2,1,0:T(8,128)(2,1)S(1)} %get-tuple-element.4.gall, f32[32,768]{1,0:T(8,128)S(1)} %get-tuple-element.5.grads_ref), custom_call_target="tpu_custom_call" | custom-call | tf_op jit(solution)/shard_map/pallas_call | solution.py:328

commit v4 on v3

--- a/solution.py
+++ b/solution.py
@@ -211,9 +211,10 @@
         total += precv[j].astype(F32)
 
     high, low = split(total)
-    grads = lax.dot_general(high, m_ref[...], NT, preferred_element_type=F32) + lax.dot_general(
-        low, m_ref[...], NT, preferred_element_type=F32
+    both = lax.dot_general(
+        jnp.concatenate([high, low], axis=0), m_ref[...], NT, preferred_element_type=F32
     )
+    grads = both[:rows] + both[rows:]
 
     def place(a_, b_, c_):
         return (c_ * B + b_) * A + a_

time: 34.9 us -> 34.6 us (level)
  Pallas kernels: 34.1 us -> 33.7 us
where the time goes in v4:
time: 34.6 us; the launch traced here: 34.4 us
  Pallas kernels  33.7 us (97%)
  between operations  0.64 us (2%)
    pallas_call x1, Pallas kernels, local(): pl.pallas_call(functools.partial(kernel, A, B), out_shape=(pltpu.VMEM((n,...  32.1 us
    pallas_call x1, Pallas kernels, local(): pl.pallas_call(finish, out_shape=(jax.ShapeDtypeStruct((width // n, width...  1.57 us

profile of v4, /device:TPU:1, one launch (start us, length us, event | category | flops | bytes accessed | tf_op | source)
XLA Modules:
  0.0 34.4 jit_solution(3937279749368359200)
XLA Ops:
  0.6 32.1 %shard_map.59 = (bf16[16,32,768]{2,1,0:T(8,128)(2,1)S(1)}, f32[32,768]{1,0:T(8,128)S(1)}) custom-call(bf16[192,768]{1,0:T(8,128)(2,1)} %c_hbm.1, s32[1,32]{1,0:T(1,128)} %bitcast.3, f32[1,192]{1,0:T(1,128)} %bitcast.2, bf16[768,768]{1,0:T(8,128)(2,1)} %m_hbm.1), custom_call_target="tpu_custom_call" | custom-call | tf_op jit(solution)/shard_map/pallas_call | solution.py:302
  32.8 1.6 %shard_map.60 = (f32[48,768]{1,0:T(8,128)}, f32[32,768]{1,0:T(8,128)}) custom-call(bf16[16,32,768]{2,1,0:T(8,128)(2,1)S(1)} %get-tuple-element.4.gall, f32[32,768]{1,0:T(8,128)S(1)} %get-tuple-element.5.grads_ref), custom_call_target="tpu_custom_call" | custom-call | tf_op jit(solution)/shard_map/pallas_call | solution.py:329
